TPU v7x, 256 devices: a whole 4x4x8 slice. The times are simulated.
256 devices in a mesh: region: 8 (over x, core), domain: 32 (over z, y).
Axes of the slice: x: 4, y: 4, z: 8, core: 2. Of those that a mesh axis runs over, the one named last changes fastest.
Arguments:
- midpoints: float32 [3, 131072], P(None, ('region', 'domain')), may hold values from 0 to 1, as said below
- line_vectors: float32 [3, 131072], P(None, ('region', 'domain')), may hold values from -0.046875 to 0.046875
- burgers: float32 [3, 131072], P(None, ('region', 'domain')), may hold values from -4 to 4
- destination: int32 [131072, 1], P(('region', 'domain')), may hold values from 0 to 31; in each aligned block of 512 rows (0 to 511, 512 to 1023, ...) at most 32 rows name the same one
- node_ids: int32 [2, 131072], P(None, ('region', 'domain')), may hold values from 0 to 8191
- cell_ids: int32 [131072], P(('region', 'domain')), may hold values from 0 to 127, as said below
- cell_centers: float32 [3, 1024], replicated, may hold values from 0 to 1, as said below
Outputs:
- slot_traction: float32 [3, 262144], P(None, ('region', 'domain'))
- nodal_force: float32 [3, 65536], P(None, ('region', 'domain'))
Inputs may be any that keep to these rules, and one draw needn't show every extreme that they name: `destination`: among the rows of one device, no domain is named by more than 32 rows, a bound that some block reaches. `cell_ids`: region r is the slab of x from r / 8 to (r + 1) / 8 of the unit cube; its 128 cells are the boxes of a 2 x 4 x (16) grid in that slab, numbered with the last grid index fastest. `cell_centers`: each cell's center lies within its box, within a quarter of the box's width of the box's middle along each dimension. `midpoints`: each segment's midpoint lies within its cell's box.
All inputs are finite; a program needn't handle non-finite values.
Results may differ from a plain program's by a relative error of at most 0.0003.
Values sent between devices are 32-bit elements; how exact they have to be, the bound alone decides.
A program may use at most 64 MiB of HBM per device.

v0:
```python
import jax
import jax.numpy as jnp
from jax import lax
from jax.sharding import Mesh
from jax.sharding import PartitionSpec as P

CELLS_REG = 128
DOMAIN = ("domain_0", "domain_1")
REGION_DOMAIN = ("region", "domain_0", "domain_1")


CORE2 = 0.01
EXACT = lax.Precision.HIGHEST


def sent_to_all(x, axis):
    size = lax.axis_size(axis)
    return lax.all_to_all(jnp.broadcast_to(x[None], (size, *x.shape)), axis, 0, 0, tiled=True)


def taken_together(x, axis):
    everything = sent_to_all(x, axis)
    return jnp.sum(everything, axis=0)


def in_order(tiles, dim):
    tiles = jnp.moveaxis(tiles, 0, dim)
    shape = tiles.shape
    return tiles.reshape(*shape[:dim], shape[dim] * shape[dim + 1], *shape[dim + 2 :])


def collect(x, axis, dim):
    tiles = sent_to_all(x, axis)
    return in_order(tiles, dim)


def whole_of(x, axes, dim):
    for axis in reversed(axes):
        x = lax.all_gather(x, axis, axis=dim, tiled=True)
    return x


def in_blocks(x, dim, size):
    shape = x.shape
    tiles = x.reshape(*shape[:dim], size, shape[dim] // size, *shape[dim + 1 :])
    return jnp.moveaxis(tiles, dim, 0)


def sum_at_owner(x, axis, dim):
    tiles = in_blocks(x, dim, lax.axis_size(axis))
    arrived = lax.all_to_all(tiles, axis, split_axis=0, concat_axis=0, tiled=True)
    return arrived.sum(axis=0)


def product(left, right):
    return jnp.dot(left, right, precision=EXACT, preferred_element_type=jnp.float32)


def source_terms(m, l, b):
    count = m.shape[1]
    outer = (b[:, None, :] * l[None, :, :]).reshape(9, count)
    q = jnp.cross(b, l, axis=0)
    qm = (q[:, None, :] * m[None, :, :]).reshape(9, count)
    return (outer, jnp.concatenate([qm, q], axis=0))


def pair_block(m, outer, second, targets):
    r2 = (targets[0][None, :] - m[0][:, None]) ** 2
    r2 = r2 + (targets[1][None, :] - m[1][:, None]) ** 2
    r2 = r2 + (targets[2][None, :] - m[2][:, None]) ** 2
    g1 = 1.0 / jnp.sqrt(r2 + CORE2)
    g3 = g1 * g1 * g1
    first = product(outer, g1)
    other = product(second, g3)
    cross_part = (other[9:12][:, None, :] * targets[None, :, :]).reshape(9, targets.shape[1])
    return first + cross_part - other[0:9]


def moment_terms(m, l, b, centers):
    count = m.shape[1]
    outer = (b[:, None, :] * l[None, :, :]).reshape(9, count)
    offset = m - centers
    dipole = (outer[:, None, :] * offset[None, :, :]).reshape(27, count)
    q = jnp.cross(b, l, axis=0)
    return jnp.concatenate([outer, dipole, q], axis=0)


def far_field(moments, centers, region_centers, region, cells_reg):
    total = centers.shape[1]
    diffs = [region_centers[a][None, :] - centers[a][:, None] for a in range(3)]
    r2 = diffs[0] ** 2 + diffs[1] ** 2 + diffs[2] ** 2
    keep = (jnp.arange(total, dtype=jnp.int32) // cells_reg != region).astype(jnp.float32)
    g1 = keep[:, None] / jnp.sqrt(r2 + CORE2)
    g3 = g1 * g1 * g1
    field = product(moments[0:9], g1)
    pulls = []
    for axis_a in range(3):
        weighted = diffs[axis_a] * g3
        field = field + product(moments[9 + axis_a : 36 : 3], weighted)
        pulls.append(product(moments[36:39], weighted))
    nterm = jnp.stack(pulls, axis=1).reshape(9, region_centers.shape[1])
    return field + nterm


def traction(stress, b):
    count = stress.shape[1]
    sigma = stress.reshape(3, 3, count)
    sym = 0.5 * (sigma + jnp.transpose(sigma, (1, 0, 2)))
    return jnp.sum(sym * b[None, :, :], axis=1)


def fold_blocks(total_stress, rows, block_fn):
    width = rows.shape[1]
    split = jnp.transpose(rows.reshape(rows.shape[0], width // 512, 512), (1, 0, 2))

    def step(carry, part):
        return (carry + block_fn(part), None)

    result, _ = lax.scan(step, total_stress, split)
    return result


def body(midpoints, line_vectors, burgers, destination, node_ids, cell_ids, cell_centers):
    count = midpoints.shape[1]
    domains = lax.axis_size(DOMAIN)
    capacity = 2 * count // domains
    slots = 2 * count
    region = lax.axis_index("region")
    region_centers = lax.dynamic_slice_in_dim(cell_centers, region * CELLS_REG, CELLS_REG, 1)
    cell_table = (jnp.arange(CELLS_REG, dtype=jnp.int32)[:, None] == cell_ids[None, :]).astype(
        jnp.float32
    )
    seg_centers = product(region_centers, cell_table)
    feats = moment_terms(midpoints, line_vectors, burgers, seg_centers)
    partial_value = product(feats, cell_table.T)
    summed = taken_together(partial_value, DOMAIN)
    moments = collect(summed, "region", 1)
    far = far_field(moments, cell_centers, region_centers, region, CELLS_REG)
    geometry = jnp.concatenate([midpoints, line_vectors, burgers], axis=0)
    dest = destination[:, 0]
    hot = (dest[:, None] == jnp.arange(domains, dtype=jnp.int32)[None, :]).astype(jnp.int32)
    rank = jnp.sum(jnp.cumsum(hot, axis=0) * hot, axis=1) - 1
    slot = dest * capacity + rank
    empty = jnp.zeros((9, midpoints.shape[1]), jnp.float32)

    def raw_block(rows):
        outer_rows, second_rows = source_terms(rows[0:3], rows[3:6], rows[6:9])
        return pair_block(rows[0:3], outer_rows, second_rows, midpoints)

    stress = fold_blocks(empty, whole_of(geometry, DOMAIN, 1), raw_block) + product(far, cell_table)
    force = traction(stress, burgers)
    outgoing = jnp.zeros((3, slots), jnp.float32).at[:, slot].set(force)
    slot_traction = lax.all_to_all(outgoing, DOMAIN, split_axis=1, concat_axis=1, tiled=True)
    half = 0.5 * force
    node_partial = jnp.zeros((3, count // 2 * domains), jnp.float32)
    node_partial = node_partial.at[:, node_ids[0]].add(half).at[:, node_ids[1]].add(half)
    nodal_force = sum_at_owner(node_partial, DOMAIN, 1)
    return (slot_traction, nodal_force)


def solution(mesh):
    split = Mesh(
        mesh.devices.reshape(mesh.shape["region"], 8, 4), ("region", "domain_0", "domain_1")
    )
    in_specs = (
        P(None, REGION_DOMAIN),
        P(None, REGION_DOMAIN),
        P(None, REGION_DOMAIN),
        P(REGION_DOMAIN, None),
        P(None, REGION_DOMAIN),
        P(REGION_DOMAIN),
        P(),
    )
    out_specs = (P(None, REGION_DOMAIN), P(None, REGION_DOMAIN))
    return jax.shard_map(body, mesh=split, in_specs=in_specs, out_specs=out_specs, check_vma=False)
```

profile of v0, /device:TPU:2, one launch (start us, length us, event | category | flops | bytes accessed | tf_op | source)
XLA Modules:
  0.0 202.6 jit_solution(11446534586697809600)
XLA Ops:
  5.7 11.5 %all-to-all-start = ((f32[32,39,128]{2,1,0:T(8,128)}), f32[32,39,128]{2,1,0:T(8,128)S(1)}, u32[]{:S(2)}, u32[]{:S(2)}) async-start(f32[32,39,128]{2,1,0:T(8,128)} %broadcast_in_dim.15), calls=%async_computation | async-start | bytes 1310720 | tf_op jit(solution)/shard_map/all_to_all | solution.py:18
  17.9 13.4 %all_gather.6 = f32[9,2048]{1,0:T(8,128)S(1)} all-gather(f32[9,512]{1,0:T(8,128)S(1)} %pad_maximum_fusion.1), channel_id=1, replica_groups=mesh['region'=8,'domain_0'=8,'domain_1'=4] {'domain_1'}, dimensions={1}, use_global_device_ids=true | all-gather | bytes 92160 | tf_op jit(solution)/shard_map/all_gather | solution.py:39
  31.3 27.7 %all_gather.7 = f32[9,16384]{1,0:T(8,128)S(1)} all-gather(f32[9,2048]{1,0:T(8,128)S(1)} %all_gather.6), channel_id=1, replica_groups=mesh['region'=8,'domain_0'=8,'domain_1'=4] {'domain_0'}, dimensions={1}, use_global_device_ids=true | all-gather | bytes 663552 | tf_op jit(solution)/shard_map/all_gather | solution.py:39
  59.7 76.5 %while.11 = (s32[]{:T(128)}, f32[9,512]{1,0:T(8,128)S(1)}, f32[32,9,512]{2,0,1:T(8,128)S(1)}, f32[3,512]{1,0:T(4,128)S(1)}, s32[]{:T(128)}, /*index=5*/s32[]{:T(128)}, s32[]{}, s32[]{}, s32[]{}, s32[]{}) while((s32[]{:T(128)}, f32[9,512]{1,0:T(8,128)S(1)}, f32[32,9,512]{2,0,1:T(8,128)S(1)}, f32[3,512]{1,0:T(4,128)S(1)}, s32[]{:T(128)}, ...), condition=%wide.region_4.6_spmd.clone, body=%wide.region_3.5_spmd.clone.sunk | while | flops 71361536 | bytes 522423 | solution.py:119
  59.9 1.1 fusion.107
  62.3 1.1 fusion.107
  67.1 1.1 fusion.107
  69.5 1.1 fusion.107
  76.7 1.1 fusion.107
  79.0 1.1 fusion.107
  83.8 1.1 fusion.107
  86.2 1.1 fusion.107
  91.0 1.1 fusion.107
  93.4 1.1 fusion.107
  98.2 1.1 fusion.107
  100.5 1.1 fusion.107
  105.3 1.1 fusion.107
  107.7 1.1 fusion.107
  112.5 1.1 fusion.107
  114.9 1.1 fusion.107
  122.1 1.1 fusion.107
  124.4 1.1 fusion.107
  136.2 1.2 reduce-window.6
  138.6 4.8 %all-to-all-start.1 = ((f32[8,39,128]{2,1,0:T(8,128)}), f32[8,39,128]{2,1,0:T(8,128)S(1)}, u32[]{:S(2)}, u32[]{:S(2)}) async-start(f32[8,39,128]{2,1,0:T(8,128)} %broadcast_in_dim.16), calls=%async_computation.1 | async-start | bytes 327680 | tf_op jit(solution)/shard_map/all_to_all | solution.py:18
  143.5 5.0 %all-to-all-done.1 = f32[8,39,128]{2,1,0:T(8,128)S(1)} async-done(((f32[8,39,128]{2,1,0:T(8,128)}), f32[8,39,128]{2,1,0:T(8,128)S(1)}, u32[]{:S(2)}, u32[]{:S(2)}) %all-to-all-start.1) | async-done | bytes 159776 | tf_op jit(solution)/shard_map/all_to_all | solution.py:18
  155.5 1.8 scatter_custom_fusion
  158.3 8.1 %all-to-all-start.2 = ((f32[3,32,32]{2,0,1:T(4,128)}), f32[3,32,32]{2,0,1:T(4,128)S(1)}, u32[]{:S(2)}, u32[]{:S(2)}) async-start(f32[3,32,32]{2,0,1:T(4,128)} %copy.71), calls=%async_computation.2 | async-start | bytes 131072 | tf_op jit(solution)/shard_map/all_to_all | solution.py:153
  166.6 4.4 %scatter_custom_fusion.1 = f32[3,8192]{0,1:T(8,128)} fusion(s32[512]{0:T(512)S(1)} %bitcast.192, f32[512,3]{1,0:T(8,128)S(1)} %copy.73, f32[]{:T(128)} %constant.24.clone.1), kind=kCustom, calls=%fused_computation.51 | custom fusion | flops 1536 | bytes 98308 | tf_op jit(solution)/shard_map/scatter-add | solution.py:156
  171.0 7.1 %scatter_fusion = f32[3,8192]{0,1:T(8,128)} fusion(f32[3,8192]{0,1:T(8,128)} %scatter_custom_fusion.1, s32[512]{0:T(512)S(1)} %bitcast.168, f32[512,3]{1,0:T(8,128)S(1)} %copy.73), kind=kCustom, calls=%fused_computation.2 | custom fusion | flops 1536 | bytes 20480 | tf_op jit(solution)/shard_map/scatter-add | solution.py:156
  178.0 3.5 %copy.75 = f32[3,32,256]{2,0,1:T(4,128)} copy(f32[3,32,256]{0,2,1:T(8,128)} %bitcast.135) | data formatting | bytes 196608 | tf_op jit(solution)/shard_map/reshape | solution.py:45
  181.5 9.8 %all-to-all-start.3 = ((f32[32,3,256]{2,1,0:T(4,128)}), f32[32,3,256]{2,1,0:T(4,128)S(1)}, u32[]{:S(2)}, u32[]{:S(2)}) async-start(f32[32,3,256]{2,1,0:T(4,128)} %bitcast.31), calls=%async_computation.3 | async-start | bytes 262144 | tf_op jit(solution)/shard_map/all_to_all | solution.py:51
  192.0 9.9 %all-to-all-done.3 = f32[32,3,256]{2,1,0:T(4,128)S(1)} async-done(((f32[32,3,256]{2,1,0:T(4,128)}), f32[32,3,256]{2,1,0:T(4,128)S(1)}, u32[]{:S(2)}, u32[]{:S(2)}) %all-to-all-start.3) | async-done | bytes 98336 | tf_op jit(solution)/shard_map/all_to_all | solution.py:51
  (565 shorter events, 70.2 us)
Async XLA Ops:
  0.6 59.1 %copy-start = (f32[3,512]{1,0:T(4,128)S(1)}, f32[3,512]{1,0:T(4,128)}, u32[]{:S(2)}) copy-start(f32[3,512]{1,0:T(4,128)} %param.11) | copy-start | bytes 18436
  5.7 132.2 %all-to-all-start = ((f32[32,39,128]{2,1,0:T(8,128)}), f32[32,39,128]{2,1,0:T(8,128)S(1)}, u32[]{:S(2)}, u32[]{:S(2)}) async-start(f32[32,39,128]{2,1,0:T(8,128)} %broadcast_in_dim.15), calls=%async_computation | async-start | bytes 1310720 | tf_op jit(solution)/shard_map/all_to_all | solution.py:18
  59.7 76.5 %copy-start.2 = (s32[512,1]{0,1:T(1,128)S(1)}, s32[512,1]{0,1:T(1,128)}, u32[]{:S(2)}) copy-start(s32[512,1]{0,1:T(1,128)} %param.14) | copy-start | bytes 6148
  59.7 78.1 %copy-start.4 = (s32[2,512]{1,0:T(2,128)S(1)}, s32[2,512]{1,0:T(2,128)}, u32[]{:S(2)}) copy-start(s32[2,512]{1,0:T(2,128)} %param.15) | copy-start | bytes 12292
  59.7 78.1 %copy-start.1 = (f32[3,512]{1,0:T(4,128)S(1)}, f32[3,512]{1,0:T(4,128)}, u32[]{:S(2)}) copy-start(f32[3,512]{1,0:T(4,128)} %param.13) | copy-start | bytes 18436
  59.7 78.1 %copy-start.3 = (f32[3,1024]{1,0:T(4,128)S(1)}, f32[3,1024]{1,0:T(4,128)}, u32[]{:S(2)}) copy-start(f32[3,1024]{1,0:T(4,128)} %param.17) | copy-start | bytes 36868
  138.6 9.9 %all-to-all-start.1 = ((f32[8,39,128]{2,1,0:T(8,128)}), f32[8,39,128]{2,1,0:T(8,128)S(1)}, u32[]{:S(2)}, u32[]{:S(2)}) async-start(f32[8,39,128]{2,1,0:T(8,128)} %broadcast_in_dim.16), calls=%async_computation.1 | async-start | bytes 327680 | tf_op jit(solution)/shard_map/all_to_all | solution.py:18
  151.4 3.8 %copy-start.5 = (s32[512]{0:T(512)S(1)}, s32[512]{0:T(512)}, u32[]{:S(2)}) copy-start(s32[512]{0:T(512)} %param.16) | copy-start | bytes 6148
  158.3 23.2 %all-to-all-start.2 = ((f32[3,32,32]{2,0,1:T(4,128)}), f32[3,32,32]{2,0,1:T(4,128)S(1)}, u32[]{:S(2)}, u32[]{:S(2)}) async-start(f32[3,32,32]{2,0,1:T(4,128)} %copy.71), calls=%async_computation.2 | async-start | bytes 131072 | tf_op jit(solution)/shard_map/all_to_all | solution.py:153
  181.5 20.4 %all-to-all-start.3 = ((f32[32,3,256]{2,1,0:T(4,128)}), f32[32,3,256]{2,1,0:T(4,128)S(1)}, u32[]{:S(2)}, u32[]{:S(2)}) async-start(f32[32,3,256]{2,1,0:T(4,128)} %bitcast.31), calls=%async_computation.3 | async-start | bytes 262144 | tf_op jit(solution)/shard_map/all_to_all | solution.py:51
where the time goes:
time: 203 us
  matrix products  76.2 us (38%)
  blocking collectives  41.1 us (20%)
  starting transfers between devices  34.2 us (17%)
  other arithmetic  17.5 us (9%)
  waiting for transfers between devices  14.9 us (7%)
  local copies, waits for them, and re-layouts  14.2 us (7%)
  loops' own time  3.38 us (2%)
    dot_general x74, matrix products, product(): jnp.dot(left, right, precision=EXACT, preferred_element_type=jnp.float32)  76.2 us
    all_gather x2, blocking collectives, whole_of(): x = lax.all_gather(x, axis, axis=dim, tiled=True)  41.1 us
    all_to_all x2, starting transfers between devices, sent_to_all(): lax.all_to_all(jnp.broadcast_to(x[None], (size, *x.shape)), axis, 0, 0, t...  16.3 us
    scatter-add x2, other arithmetic, body(): node_partial.at[:, node_ids[0]].add(half).at[:, node_ids[1]].add(half)  11.5 us
    all_to_all x1, waiting for transfers between devices, sum_at_owner(): lax.all_to_all(tiles, axis, split_axis=0, concat_axis=0, tiled=True)  9.92 us
    all_to_all x1, starting transfers between devices, sum_at_owner(): lax.all_to_all(tiles, axis, split_axis=0, concat_axis=0, tiled=True)  9.78 us
    all_to_all x1, starting transfers between devices, body(): lax.all_to_all(outgoing, DOMAIN, split_axis=1, concat_axis=1, tiled=True)  8.11 us
    all_to_all x2, waiting for transfers between devices, sent_to_all(): lax.all_to_all(jnp.broadcast_to(x[None], (size, *x.shape)), axis, 0, 0, t...  5.02 us
  transfers between devices with their start and end apart: 4, of which 2 were waited for; matrix products, arithmetic and copies ran while one was open for 45% of the time, Pallas kernels for 0%

commit v1 on v0

v1 whole, which is shorter than its diff:
```python
import jax
import jax.numpy as jnp
from jax import lax
from jax.experimental import pallas as pl
from jax.experimental.pallas import tpu as pltpu
from jax.sharding import PartitionSpec as P

MESH = pl.DeviceIdType.MESH
F32, BF16, I32 = jnp.float32, jnp.bfloat16, jnp.int32
CORE2 = 0.01
REGIONS, DOMAINS, NZ, NY = 8, 32, 8, 4
SEG, TILE, CHUNK, LANES = 512, 256, 64, 128
CHUNKS = SEG // CHUNK


def split2(v):
    high = v.astype(BF16)
    return high, (v - high.astype(F32)).astype(BF16)


def split3(v):
    high = v.astype(BF16)
    rest = v - high.astype(F32)
    mid = rest.astype(BF16)
    return high, mid, (rest - mid.astype(F32)).astype(BF16)


def cross(b, l):
    return [b[1] * l[2] - b[2] * l[1], b[2] * l[0] - b[0] * l[2], b[0] * l[1] - b[1] * l[0]]


def rows_of(ref):
    return [ref[a : a + 1, :] for a in range(3)]


def mxu_sum(rows, steps):
    def run(*accs):
        for n, (left, right, turned) in enumerate(steps):
            unit, stage = n % 2, n // 2 % 2
            pltpu.matmul_push_rhs(right, stage, unit, transpose=turned)
            pltpu.matmul_acc_lhs(accs[unit], left, stage)
        total = pltpu.matmul_pop(accs[0])
        return total + pltpu.matmul_pop(accs[1]) if len(steps) > 1 else total

    return pl.run_scoped(run, *[pltpu.ACC(w)((rows, TILE), F32) for w in range(2)])


def padded(right):
    return jnp.concatenate([right, jnp.zeros((TILE - right.shape[0], right.shape[1]), right.dtype)], axis=0)


def dot_nt(left, right):
    tiles = [slice(k, k + TILE) for k in range(0, left.shape[1], TILE)]
    return mxu_sum(left.shape[0], [(left[:, k], padded(right[:, k]), True) for k in tiles])


def offset(k, z, y):
    i = k // NY
    odd = i % 2
    dz = odd * ((i + 1) // 2) + (1 - odd) * ((NZ - i // 2) % NZ)
    return ((z + dz) % NZ) * NY + (y + k % NY) % NY


def kernel(
    mid, lin, bur, dest, nid, cid, cen,
    slot_out, node_out,
    geo, xb, wsc, mom, my_in, mz_in, mall, msg, arrived, nodehot, rankhot, desthot,
    geo_send, geo_recv, my_send, my_recv, mz_send, mz_recv, mr_send, mr_recv, out_send, out_recv,
):
    region, dom = lax.axis_index("region"), lax.axis_index("domain")
    z, y = dom // NY, dom % NY

    barrier = pltpu.get_barrier_semaphore()

    def greet_domain(k, c):
        pl.semaphore_signal(barrier, inc=1, device_id=(region, (dom + k) % DOMAINS), device_id_type=MESH)
        return c

    def greet_region(k, c):
        pl.semaphore_signal(barrier, inc=1, device_id=((region + k) % REGIONS, dom), device_id_type=MESH)
        return c

    lax.fori_loop(1, DOMAINS, greet_domain, 0)
    lax.fori_loop(1, REGIONS, greet_region, 0)

    def empty(*accs):
        for acc in accs:
            pltpu.matmul_pop(acc)

    pl.run_scoped(empty, *[pltpu.ACC(w)((SEG, TILE), F32) for w in range(2)])

    middle = [(region.astype(F32) + 0.5) / REGIONS, 0.5, 0.5]
    m = [mid[a : a + 1, :] - middle[a] for a in range(3)]
    l, b = rows_of(lin), rows_of(bur)
    for c, row in enumerate(m + l + b):
        for j in range(4):
            geo[0, 4 * c + j : 4 * c + j + 1, :] = row[:, j * LANES : (j + 1) * LANES]
    for j in range(4):
        geo[0, 36 + j : 37 + j, :] = jnp.zeros((1, LANES), F32)

    outer = [b[i] * l[j] for i in range(3) for j in range(3)]
    q = cross(b, l)
    zero = jnp.zeros((1, SEG), F32)
    feats = outer + [outer[k] * m[a] for a in range(3) for k in range(9)]
    feats = jnp.concatenate(feats + q + [zero], axis=0)
    cell_hot = (lax.broadcasted_iota(I32, (LANES, SEG), 0) == cid[...]).astype(F32).astype(BF16)
    feats = [jnp.concatenate([part, jnp.zeros((8, SEG), BF16)], axis=0) for part in split3(feats)]
    parts = dot_nt(jnp.concatenate(feats, axis=0), cell_hot)[:, 0:LANES]
    mom[...] = parts[0:40] + parts[48:88] + parts[96:136]

    pl.semaphore_wait(barrier, DOMAINS - 1 + REGIONS - 1)

    def y_copy(k):
        return pltpu.make_async_remote_copy(
            src_ref=mom, dst_ref=my_in.at[k], send_sem=my_send.at[k], recv_sem=my_recv.at[k],
            device_id=(region, z * NY + (y + k) % NY), device_id_type=MESH)

    def geo_copy(k):
        return pltpu.make_async_remote_copy(
            src_ref=geo.at[0], dst_ref=geo.at[k], send_sem=geo_send.at[k], recv_sem=geo_recv.at[k],
            device_id=(region, offset(k, z, y)), device_id_type=MESH)

    def z_copy(k):
        return pltpu.make_async_remote_copy(
            src_ref=mz_in.at[0], dst_ref=mz_in.at[k], send_sem=mz_send.at[k], recv_sem=mz_recv.at[k],
            device_id=(region, ((z + k) % NZ) * NY + y), device_id_type=MESH)

    def r_copy(k):
        return pltpu.make_async_remote_copy(
            src_ref=mall.at[0], dst_ref=mall.at[k], send_sem=mr_send.at[k], recv_sem=mr_recv.at[k],
            device_id=((region + k) % REGIONS, dom), device_id_type=MESH)

    def start(copy):
        def run(k, c):
            copy(k).start()
            return c

        return run

    for k in range(1, NY):
        y_copy(k).start()
    lax.fori_loop(1, DOMAINS, start(geo_copy), 0)

    d = dest[...]
    hot = (lax.broadcasted_iota(I32, (DOMAINS, SEG), 0) == d).astype(F32)
    upper = lax.broadcasted_iota(I32, (TILE, TILE), 0) < lax.broadcasted_iota(I32, (TILE, TILE), 1)
    upper = upper.astype(F32).astype(BF16)
    first, second = hot[:, 0:TILE].astype(BF16), hot[:, TILE:SEG].astype(BF16)
    ones = jnp.ones((TILE, TILE), BF16)
    before = jnp.concatenate(
        [mxu_sum(DOMAINS, [(first, upper, False)]), mxu_sum(DOMAINS, [(second, upper, False), (first, ones, False)])], axis=1
    )
    rank = jnp.sum(before * hot, axis=0, keepdims=True)
    desthot[...] = hot
    rankhot[...] = (lax.broadcasted_iota(I32, (DOMAINS, SEG), 0).astype(F32) == rank).astype(F32).astype(BF16)
    for e in range(2):
        low = nid[e : e + 1, :] & (LANES - 1)
        nodehot[:, e * SEG : (e + 1) * SEG] = (lax.broadcasted_iota(I32, (LANES, SEG), 0) == low).astype(F32).astype(BF16)

    own = jnp.concatenate([-2.0 * m[a] for a in range(3)] + [m[0] * m[0] + m[1] * m[1] + m[2] * m[2] + CORE2] + [zero] * 4, axis=0)
    columns = jnp.transpose(own)
    for a in range(4):
        xb[a] = jnp.broadcast_to(columns[:, a : a + 1], (SEG, LANES))
    wsc[...] = jnp.zeros_like(wsc)

    def pairs(*accs):
        acc1, acc3 = accs[:CHUNKS], accs[CHUNKS:]
        blank = jnp.zeros((TILE - 32, TILE), BF16)

        def block(k):
            v = [geo[k, 4 * c : 4 * c + 4, :] for c in range(9)]
            vm, vl, vb = v[0:3], v[3:6], v[6:9]
            vq = cross(vb, vl)
            for i in range(3):
                for j in range(3):
                    at = 4 * (3 * i + j)
                    wsc[0, at : at + 4, :] = vb[i] * vl[j]
                    wsc[1, at : at + 4, :] = vq[i] * vm[j]
                wsc[1, 36 + 4 * i : 40 + 4 * i, :] = vq[i]
            for t in range(2):
                for w in range(2):
                    wide = jnp.concatenate([wsc[w, pl.ds(2 * t + u, 16, stride=4), :] for u in range(2)], axis=1)
                    high, low = split2(wide)
                    pltpu.matmul_push_rhs(jnp.concatenate([high, low, blank], axis=0), 0, w, transpose=True)
                s = [
                    jnp.concatenate([geo[k, 4 * a + 2 * t + u : 4 * a + 2 * t + u + 1, :] for u in range(2)], axis=1)
                    for a in range(3)
                ]
                s2 = s[0] * s[0] + s[1] * s[1] + s[2] * s[2]
                for c in range(CHUNKS):
                    x = [jnp.concatenate([xb[a, c * CHUNK : (c + 1) * CHUNK, :]] * 2, axis=1) for a in range(4)]
                    g1 = lax.rsqrt((x[3] + s2) + x[0] * s[0] + x[1] * s[1] + x[2] * s[2])
                    h1, l1 = split2(g1)
                    h3, l3 = split2(g1 * g1 * g1)
                    first = 0 if c == 0 else None
                    pltpu.matmul_acc_lhs(acc1[c], h1, first)
                    pltpu.matmul_acc_lhs(acc3[c], h3, first)
                    pltpu.matmul_acc_lhs(acc1[c], l1)
                    pltpu.matmul_acc_lhs(acc3[c], l3)

        def arrived_block(k, carry):
            geo_copy(k).wait_recv()
            block(k)
            return carry

        block(0)
        for k in range(1, NY):
            y_copy(k).wait_recv()
        mz_in[0] = mom[...] + my_in[1] + my_in[2] + my_in[3]
        for k in range(1, NZ):
            z_copy(k).start()
        lax.fori_loop(1, 10, arrived_block, 0)
        for k in range(1, NZ):
            z_copy(k).wait_recv()
        total = mz_in[0]
        for k in range(1, NZ):
            total = total + mz_in[k]
        center = [cen[a : a + 1, pl.ds(pl.multiple_of(region * LANES, LANES), LANES)] - middle[a] for a in range(3)]
        mall[0, 0:9, :] = total[0:9]
        for a in range(3):
            for k in range(9):
                at = 9 + 9 * a + k
                value = total[at : at + 1] - center[a] * total[k : k + 1]
                if k % 3 == a:
                    value = value + total[36 + k // 3 : 37 + k // 3]
                mall[0, at : at + 1, :] = value
        mall[0, 36:40, :] = jnp.zeros((4, LANES), F32)
        for k in range(1, REGIONS):
            r_copy(k).start()
        lax.fori_loop(10, DOMAINS, arrived_block, 0)
        for c in range(CHUNKS):
            one, three = pltpu.matmul_pop(acc1[c]), pltpu.matmul_pop(acc3[c])
            xb[0, c * CHUNK : (c + 1) * CHUNK, :] = one[:, 0:LANES]
            xb[1, c * CHUNK : (c + 1) * CHUNK, :] = three[:, 0:LANES]

    pl.run_scoped(pairs, *[pltpu.ACC(w)((CHUNK, TILE), F32) for w in range(2) for _ in range(CHUNKS)])

    for k in range(1, REGIONS):
        r_copy(k).wait_recv()
    at = pl.ds(pl.multiple_of(region * LANES, LANES), LANES)
    target = jnp.transpose(jnp.concatenate([cen[0:3, at], jnp.zeros((5, LANES), F32)], axis=0))
    target = [jnp.broadcast_to(target[:, a : a + 1], (LANES, LANES)) for a in range(3)]
    weights, kernels = [], []
    for k in range(1, REGIONS):
        source = pl.ds(pl.multiple_of(((region + REGIONS - k) % REGIONS) * LANES, LANES), LANES)
        diff = [target[a] - cen[a : a + 1, source] for a in range(3)]
        g1 = lax.rsqrt(diff[0] * diff[0] + diff[1] * diff[1] + diff[2] * diff[2] + CORE2)
        g3 = g1 * g1 * g1
        total = mall[k]
        for p, part in enumerate([g1] + [diff[a] * g3 for a in range(3)]):
            high, low = split2(part)
            wh, wl = split2(jnp.concatenate([total[9 * p : 9 * p + 9], jnp.zeros((7, LANES), F32)], axis=0))
            both = jnp.concatenate([wh, wl], axis=0)
            kernels += [high, low]
            weights += [both, both]
    far = dot_nt(jnp.concatenate(weights, axis=1), jnp.concatenate(kernels, axis=1))
    far = split3(far[0:16, 0:LANES] + far[16:32, 0:LANES])
    cell_hot = (lax.broadcasted_iota(I32, (TILE, SEG), 0) % LANES == cid[...]).astype(F32).astype(BF16)
    pair = [jnp.concatenate(far[0:2], axis=1), jnp.concatenate([far[2], jnp.zeros_like(far[2])], axis=1)]
    far = jnp.concatenate(
        [mxu_sum(16, [(left, cell_hot[:, k : k + TILE], False) for left in pair]) for k in (0, TILE)], axis=1
    )

    one, three = jnp.transpose(xb[0]), jnp.transpose(xb[1])
    one = one[0:16] + one[16:32]
    three = three[0:16] + three[16:32]
    x = [mid[a : a + 1, :] - middle[a] for a in range(3)]
    b = rows_of(bur)
    stress = [
        one[k : k + 1] + far[k : k + 1] + three[9 + k // 3 : 10 + k // 3] * x[k % 3] - three[k : k + 1] for k in range(9)
    ]
    force = []
    for i in range(3):
        total = zero
        for j in range(3):
            total = total + 0.5 * (stress[3 * i + j] + stress[3 * j + i]) * b[j]
        force.append(total)

    halves = [0.5 * f for f in force]
    table = jnp.concatenate([halves[0]] * 2 + [halves[1]] * 2 + [halves[2]] * 2 + [zero] * 2, axis=0)
    table_high = table.astype(BF16).astype(F32)
    table_low = table - table_high
    sub = lax.broadcasted_iota(I32, (8, SEG), 0) % 2
    lefts = []
    for e in range(2):
        row = (nid[e : e + 1, :] // LANES) - sub
        hits = [row == 2 * owner for owner in range(DOMAINS)]
        for part in (table_high, table_low):
            lefts.append(jnp.concatenate([jnp.where(hit, part, 0.0) for hit in hits], axis=0).astype(BF16))
    rights = [nodehot[:, e * SEG : (e + 1) * SEG] for e in (0, 0, 1, 1)]
    nodes = dot_nt(jnp.concatenate(lefts, axis=1), jnp.concatenate(rights, axis=1))
    hot = desthot[...]
    left = [part for c in range(3) for part in split3(hot * force[c])]
    part = dot_nt(jnp.concatenate(left, axis=0), rankhot[...])[:, 0:32]
    slots = [part[96 * c : 96 * c + 32] + part[96 * c + 32 : 96 * c + 64] + part[96 * c + 64 : 96 * c + 96] for c in range(3)]
    slots = jnp.concatenate(slots + [jnp.zeros((DOMAINS, 32), F32)], axis=1)
    msg[...] = nodes[:, 0:LANES]
    msg[pl.ds(6, DOMAINS, stride=8), :] = slots

    def out_copy(k):
        peer = (dom + k) % DOMAINS
        return pltpu.make_async_remote_copy(
            src_ref=msg.at[pl.ds(pl.multiple_of(8 * peer, 8), 8), :],
            dst_ref=arrived.at[pl.ds(pl.multiple_of(8 * dom, 8), 8), :],
            send_sem=out_send.at[k], recv_sem=out_recv.at[k],
            device_id=(region, peer), device_id_type=MESH)

    lax.fori_loop(1, DOMAINS, start(out_copy), 0)
    mine = pl.ds(pl.multiple_of(8 * dom, 8), 8)
    arrived[mine, :] = msg[mine, :]

    def received(k, c):
        out_copy(k).wait_recv()
        return c

    lax.fori_loop(1, DOMAINS, received, 0)
    total = arrived[0:8, :]
    for s in range(1, DOMAINS):
        total = total + arrived[8 * s : 8 * s + 8, :]
    for c in range(3):
        for h in range(2):
            node_out[c : c + 1, h * LANES : (h + 1) * LANES] = total[2 * c + h : 2 * c + h + 1]
    quarter = lax.broadcasted_iota(I32, (8, LANES), 1) // 32
    four = [arrived[pl.ds(6 + 8 * a, 8, stride=32), :] for a in range(4)]
    for c in range(3):
        line = jnp.zeros((8, LANES), F32)
        for a in range(4):
            turn = (32 * (a - c)) % LANES
            line = jnp.where(quarter == a, pltpu.roll(four[a], turn, 1) if turn else four[a], line)
        for j in range(8):
            slot_out[c : c + 1, j * LANES : (j + 1) * LANES] = line[j : j + 1]

    for copy, count in ((y_copy, NY), (geo_copy, DOMAINS), (z_copy, NZ), (r_copy, REGIONS), (out_copy, DOMAINS)):

        def sent(k, c, copy=copy):
            copy(k).wait_send()
            return c

        lax.fori_loop(1, count, sent, 0)


def body(midpoints, line_vectors, burgers, destination, node_ids, cell_ids, cell_centers):
    vmem = pl.BlockSpec(memory_space=pltpu.VMEM)
    dma = pltpu.SemaphoreType.DMA
    return pl.pallas_call(
        kernel,
        out_shape=(jax.ShapeDtypeStruct((3, 2 * SEG), F32), jax.ShapeDtypeStruct((3, 256), F32)),
        in_specs=[vmem] * 7,
        out_specs=(vmem, vmem),
        scratch_shapes=[
            pltpu.VMEM((DOMAINS, 40, LANES), F32),
            pltpu.VMEM((4, SEG, LANES), F32),
            pltpu.VMEM((2, 64, LANES), F32),
            pltpu.VMEM((40, LANES), F32),
            pltpu.VMEM((NY, 40, LANES), F32),
            pltpu.VMEM((NZ, 40, LANES), F32),
            pltpu.VMEM((REGIONS, 40, LANES), F32),
            pltpu.VMEM((DOMAINS * 8, LANES), F32),
            pltpu.VMEM((DOMAINS * 8, LANES), F32),
            pltpu.VMEM((LANES, 2 * SEG), BF16),
            pltpu.VMEM((DOMAINS, SEG), BF16),
            pltpu.VMEM((DOMAINS, SEG), F32),
            dma((DOMAINS,)), dma((DOMAINS,)), dma((NY,)), dma((NY,)), dma((NZ,)), dma((NZ,)),
            dma((REGIONS,)), dma((REGIONS,)), dma((DOMAINS,)), dma((DOMAINS,)),
        ],
        compiler_params=pltpu.CompilerParams(
            collective_id=0, has_side_effects=True, vmem_limit_bytes=32 << 20
        ),
    )(
        midpoints, line_vectors, burgers, destination.reshape(1, SEG), node_ids, cell_ids.reshape(1, SEG), cell_centers
    )


def solution(mesh):
    both = ("region", "domain")

    def program(*args):
        with jax.sharding.use_abstract_mesh(mesh.abstract_mesh):
            return jax.shard_map(
                body,
                mesh=mesh,
                in_specs=(P(None, both), P(None, both), P(None, both), P(both, None), P(None, both), P(both), P()),
                out_specs=(P(None, both), P(None, both)),
                check_vma=False,
            )(*args)

    return program
```

time: 203 us -> 62.6 us (0.31)
  matrix products: 76.2 us -> 0 us
  Pallas kernels: 0 us -> 55.3 us
  blocking collectives: 41.1 us -> 0 us
  starting transfers between devices: 34.2 us -> 0 us
  other arithmetic: 17.5 us -> 0 us
  waiting for transfers between devices: 14.9 us -> 0 us
  local copies, waits for them, and re-layouts: 14.2 us -> 6.05 us
  loops' own time: 3.38 us -> 0 us
    dot_general x74 -> x0, matrix products: 76.2 us -> none  [product(): jnp.dot(left, right, precision=EXACT, preferred_element_type=jnp.float32)]
    pallas_call x0 -> x1, Pallas kernels: none -> 55.3 us  [body(): pl.pallas_call(kernel, out_shape=(jax.ShapeDtypeStruct((3, 2 * SEG), F32)...]
    all_gather x2 -> x0, blocking collectives: 41.1 us -> none  [whole_of(): x = lax.all_gather(x, axis, axis=dim, tiled=True)]
    all_to_all x4 -> x0, starting transfers between devices: 34.2 us -> none  [the longest x2 16.3 us: sent_to_all(): lax.all_to_all(jnp.broadcast_to(x[None], (size, *x.shape)), axis, 0, 0, t...]
    all_to_all x4 -> x0, waiting for transfers between devices: 14.9 us -> none  [the longest x1 9.92 us: sum_at_owner(): lax.all_to_all(tiles, axis, split_axis=0, concat_axis=0, tiled=True)]
    scatter-add x2 -> x0, other arithmetic: 11.5 us -> none  [body(): node_partial.at[:, node_ids[0]].add(half).at[:, node_ids[1]].add(half)]
    unnamed x17 -> x16, local copies, waits for them, and re-layouts: 0.72 us -> 6.05 us
    reshape x3 -> x0, local copies, waits for them, and re-layouts: 3.48 us -> none  [the longest x1 3.45 us: in_blocks(): tiles = x.reshape(*shape[:dim], size, shape[dim] // size, *shape[dim + 1:])]
  transfers between devices with their start and end apart: 4 -> 0, of which waited for: 2 -> 0; matrix products, arithmetic and copies ran while one was open for 45% -> 0% of each run, Pallas kernels for 0% -> 0%
where the time goes in v1:
time: 62.6 us; the launch traced here: 62 us
  Pallas kernels  55.3 us (88%)
  local copies, waits for them, and re-layouts  6.05 us (10%)
  between operations  0.66 us (1%)
    pallas_call x1, Pallas kernels, body(): pl.pallas_call(kernel, out_shape=(jax.ShapeDtypeStruct((3, 2 * SEG), F32)...  55.3 us
    unnamed x16, local copies, waits for them, and re-layouts  6.05 us

profile of v1, /device:TPU:2, one launch (start us, length us, event | category | flops | bytes accessed | tf_op | source)
XLA Modules:
  0.0 62.0 jit_solution(9125045041561869046)
XLA Ops:
  0.6 0.0 copy-start.5
  0.6 0.7 %copy-done.5 = s32[512,1]{0,1:T(1,128)S(1)} copy-done((s32[512,1]{0,1:T(1,128)S(1)}, s32[512,1]{0,1:T(1,128)}, u32[]{:S(2)}) %copy-start.5) | copy-done | bytes 2072
  1.3 0.0 copy-start
  1.3 0.7 %copy-done = f32[3,1024]{1,0:T(4,128)S(1)} copy-done((f32[3,1024]{1,0:T(4,128)S(1)}, f32[3,1024]{1,0:T(4,128)}, u32[]{:S(2)}) %copy-start) | copy-done | bytes 12312
  2.0 0.0 copy-start.1
  2.0 0.7 %copy-done.1 = f32[3,512]{1,0:T(4,128)S(1)} copy-done((f32[3,512]{1,0:T(4,128)S(1)}, f32[3,512]{1,0:T(4,128)}, u32[]{:S(2)}) %copy-start.1) | copy-done | bytes 6168
  2.7 0.0 copy-start.2
  2.7 0.7 %copy-done.2 = f32[3,512]{1,0:T(4,128)S(1)} copy-done((f32[3,512]{1,0:T(4,128)S(1)}, f32[3,512]{1,0:T(4,128)}, u32[]{:S(2)}) %copy-start.2) | copy-done | bytes 6168
  3.4 0.0 copy-start.3
  3.4 0.7 %copy-done.3 = f32[3,512]{1,0:T(4,128)S(1)} copy-done((f32[3,512]{1,0:T(4,128)S(1)}, f32[3,512]{1,0:T(4,128)}, u32[]{:S(2)}) %copy-start.3) | copy-done | bytes 6168
  4.1 0.0 copy-start.4
  4.1 0.7 %copy-done.4 = s32[2,512]{1,0:T(2,128)S(1)} copy-done((s32[2,512]{1,0:T(2,128)S(1)}, s32[2,512]{1,0:T(2,128)}, u32[]{:S(2)}) %copy-start.4) | copy-done | bytes 4120
  4.8 0.0 copy-start.6
  4.8 0.7 %copy-done.6 = s32[512]{0:T(512)S(1)} copy-done((s32[512]{0:T(512)S(1)}, s32[512]{0:T(512)}, u32[]{:S(2)}) %copy-start.6) | copy-done | bytes 2072
  5.5 55.3 %shard_map.86 = (f32[3,1024]{1,0:T(4,128)S(1)}, f32[3,256]{1,0:T(4,128)S(1)}) custom-call(f32[3,512]{1,0:T(4,128)S(1)} %copy-done.1, f32[3,512]{1,0:T(4,128)S(1)} %copy-done.2, f32[3,512]{1,0:T(4,128)S(1)} %copy-done.3, s32[1,512]{1,0:T(1,128)S(1)} %bitcast.2, s32[2,512]{1,0:T(2,128)S(1)} %copy-done.4, s32[1,512]{1,0:T(1,128)S(1)} %bitcast.3, ...), custom_call_target="tpu_custom_call" | custom-call | tf_op jit(solution)/shard_map/pallas_call | solution.py:345
  60.8 0.6 copy.11
  61.4 0.6 copy.12
Async XLA Ops:
  0.6 0.7 %copy-start.5 = (s32[512,1]{0,1:T(1,128)S(1)}, s32[512,1]{0,1:T(1,128)}, u32[]{:S(2)}) copy-start(s32[512,1]{0,1:T(1,128)} %param.10) | copy-start | bytes 6148
  1.3 0.7 %copy-start = (f32[3,1024]{1,0:T(4,128)S(1)}, f32[3,1024]{1,0:T(4,128)}, u32[]{:S(2)}) copy-start(f32[3,1024]{1,0:T(4,128)} %cen.1) | copy-start | bytes 36868
  2.0 0.7 %copy-start.1 = (f32[3,512]{1,0:T(4,128)S(1)}, f32[3,512]{1,0:T(4,128)}, u32[]{:S(2)}) copy-start(f32[3,512]{1,0:T(4,128)} %mid.1) | copy-start | bytes 18436
  2.7 0.7 %copy-start.2 = (f32[3,512]{1,0:T(4,128)S(1)}, f32[3,512]{1,0:T(4,128)}, u32[]{:S(2)}) copy-start(f32[3,512]{1,0:T(4,128)} %lin.1) | copy-start | bytes 18436
  3.4 0.7 %copy-start.3 = (f32[3,512]{1,0:T(4,128)S(1)}, f32[3,512]{1,0:T(4,128)}, u32[]{:S(2)}) copy-start(f32[3,512]{1,0:T(4,128)} %bur.1) | copy-start | bytes 18436
  4.1 0.7 %copy-start.4 = (s32[2,512]{1,0:T(2,128)S(1)}, s32[2,512]{1,0:T(2,128)}, u32[]{:S(2)}) copy-start(s32[2,512]{1,0:T(2,128)} %nid.1) | copy-start | bytes 12292
  4.8 0.7 %copy-start.6 = (s32[512]{0:T(512)S(1)}, s32[512]{0:T(512)}, u32[]{:S(2)}) copy-start(s32[512]{0:T(512)} %param.12) | copy-start | bytes 6148

commit v2 on v1

--- a/solution.py
+++ b/solution.py
@@ -62,8 +62,9 @@
 
 
 def kernel(
-    mid, lin, bur, dest, nid, cid, cen,
+    mid_in, lin_in, bur_in, dest_in, nid_in, cid_in, cen_in,
     slot_out, node_out,
+    mid, lin, bur, dest, nid, cid, cen, in_sem, kern,
     geo, xb, wsc, mom, my_in, mz_in, mall, msg, arrived, nodehot, rankhot, desthot,
     geo_send, geo_recv, my_send, my_recv, mz_send, mz_recv, mr_send, mr_recv, out_send, out_recv,
 ):
@@ -83,11 +84,19 @@
     lax.fori_loop(1, DOMAINS, greet_domain, 0)
     lax.fori_loop(1, REGIONS, greet_region, 0)
 
+    pairs_in = zip((mid_in, lin_in, bur_in, dest_in, nid_in, cid_in, cen_in), (mid, lin, bur, dest, nid, cid, cen))
+    loads = [pltpu.make_async_copy(there, here, in_sem.at[n]) for n, (there, here) in enumerate(pairs_in)]
+    for load in loads:
+        load.start()
+
     def empty(*accs):
         for acc in accs:
             pltpu.matmul_pop(acc)
 
     pl.run_scoped(empty, *[pltpu.ACC(w)((SEG, TILE), F32) for w in range(2)])
+
+    for load in loads:
+        load.wait()
 
     middle = [(region.astype(F32) + 0.5) / REGIONS, 0.5, 0.5]
     m = [mid[a : a + 1, :] - middle[a] for a in range(3)]
@@ -108,8 +117,6 @@
     parts = dot_nt(jnp.concatenate(feats, axis=0), cell_hot)[:, 0:LANES]
     mom[...] = parts[0:40] + parts[48:88] + parts[96:136]
 
-    pl.semaphore_wait(barrier, DOMAINS - 1 + REGIONS - 1)
-
     def y_copy(k):
         return pltpu.make_async_remote_copy(
             src_ref=mom, dst_ref=my_in.at[k], send_sem=my_send.at[k], recv_sem=my_recv.at[k],
@@ -136,10 +143,6 @@
             return c
 
         return run
-
-    for k in range(1, NY):
-        y_copy(k).start()
-    lax.fori_loop(1, DOMAINS, start(geo_copy), 0)
 
     d = dest[...]
     hot = (lax.broadcasted_iota(I32, (DOMAINS, SEG), 0) == d).astype(F32)
@@ -163,53 +166,84 @@
         xb[a] = jnp.broadcast_to(columns[:, a : a + 1], (SEG, LANES))
     wsc[...] = jnp.zeros_like(wsc)
 
+    at = pl.ds(pl.multiple_of(region * LANES, LANES), LANES)
+    target = jnp.transpose(jnp.concatenate([cen[0:3, at], jnp.zeros((5, LANES), F32)], axis=0))
+    target = [jnp.broadcast_to(target[:, a : a + 1], (LANES, LANES)) for a in range(3)]
+    for k in range(1, REGIONS):
+        source = pl.ds(pl.multiple_of(((region + REGIONS - k) % REGIONS) * LANES, LANES), LANES)
+        diff = [target[a] - cen[a : a + 1, source] for a in range(3)]
+        g1 = lax.rsqrt(diff[0] * diff[0] + diff[1] * diff[1] + diff[2] * diff[2] + CORE2)
+        g3 = g1 * g1 * g1
+        for p, part in enumerate([g1] + [diff[a] * g3 for a in range(3)]):
+            kern[4 * (k - 1) + p] = jnp.concatenate(split2(part), axis=1)
+
     def pairs(*accs):
         acc1, acc3 = accs[:CHUNKS], accs[CHUNKS:]
         blank = jnp.zeros((TILE - 32, TILE), BF16)
 
-        def block(k):
+        def prepare(k, slot):
             v = [geo[k, 4 * c : 4 * c + 4, :] for c in range(9)]
             vm, vl, vb = v[0:3], v[3:6], v[6:9]
             vq = cross(vb, vl)
             for i in range(3):
                 for j in range(3):
                     at = 4 * (3 * i + j)
-                    wsc[0, at : at + 4, :] = vb[i] * vl[j]
-                    wsc[1, at : at + 4, :] = vq[i] * vm[j]
-                wsc[1, 36 + 4 * i : 40 + 4 * i, :] = vq[i]
-            for t in range(2):
-                for w in range(2):
-                    wide = jnp.concatenate([wsc[w, pl.ds(2 * t + u, 16, stride=4), :] for u in range(2)], axis=1)
-                    high, low = split2(wide)
-                    pltpu.matmul_push_rhs(jnp.concatenate([high, low, blank], axis=0), 0, w, transpose=True)
-                s = [
-                    jnp.concatenate([geo[k, 4 * a + 2 * t + u : 4 * a + 2 * t + u + 1, :] for u in range(2)], axis=1)
-                    for a in range(3)
-                ]
-                s2 = s[0] * s[0] + s[1] * s[1] + s[2] * s[2]
-                for c in range(CHUNKS):
-                    x = [jnp.concatenate([xb[a, c * CHUNK : (c + 1) * CHUNK, :]] * 2, axis=1) for a in range(4)]
-                    g1 = lax.rsqrt((x[3] + s2) + x[0] * s[0] + x[1] * s[1] + x[2] * s[2])
-                    h1, l1 = split2(g1)
-                    h3, l3 = split2(g1 * g1 * g1)
-                    first = 0 if c == 0 else None
-                    pltpu.matmul_acc_lhs(acc1[c], h1, first)
-                    pltpu.matmul_acc_lhs(acc3[c], h3, first)
-                    pltpu.matmul_acc_lhs(acc1[c], l1)
-                    pltpu.matmul_acc_lhs(acc3[c], l3)
-
-        def arrived_block(k, carry):
-            geo_copy(k).wait_recv()
-            block(k)
+                    wsc[slot, 0, at : at + 4, :] = vb[i] * vl[j]
+                    wsc[slot, 1, at : at + 4, :] = vq[i] * vm[j]
+                wsc[slot, 1, 36 + 4 * i : 40 + 4 * i, :] = vq[i]
+
+        def push(slot, t):
+            for w in range(2):
+                wide = jnp.concatenate([wsc[slot, w, pl.ds(2 * t + u, 16, stride=4), :] for u in range(2)], axis=1)
+                high, low = split2(wide)
+                pltpu.matmul_push_rhs(jnp.concatenate([high, low, blank], axis=0), t, w, transpose=True)
+
+        def stream(k, t):
+            s = [
+                jnp.concatenate([geo[k, 4 * a + 2 * t + u : 4 * a + 2 * t + u + 1, :] for u in range(2)], axis=1)
+                for a in range(3)
+            ]
+            s2 = s[0] * s[0] + s[1] * s[1] + s[2] * s[2]
+            for c in range(CHUNKS):
+                x = [jnp.concatenate([xb[a, c * CHUNK : (c + 1) * CHUNK, :]] * 2, axis=1) for a in range(4)]
+                g1 = lax.rsqrt((x[3] + s2) + x[0] * s[0] + x[1] * s[1] + x[2] * s[2])
+                h1, l1 = split2(g1)
+                h3, l3 = split2(g1 * g1 * g1)
+                first = t if c == 0 else None
+                pltpu.matmul_acc_lhs(acc1[c], h1, first)
+                pltpu.matmul_acc_lhs(acc3[c], h3, first)
+                pltpu.matmul_acc_lhs(acc1[c], l1)
+                pltpu.matmul_acc_lhs(acc3[c], l3)
+
+        def block(k, carry):
+            push(k % 2, 1)
+            stream(k, 0)
+            geo_copy(k + 1).wait_recv()
+            prepare(k + 1, (k + 1) % 2)
+            push((k + 1) % 2, 0)
+            stream(k, 1)
             return carry
 
-        block(0)
+        prepare(0, 0)
+        push(0, 0)
+        push(0, 1)
+        stream(0, 0)
+        stream(0, 1)
+
+        pl.semaphore_wait(barrier, DOMAINS - 1 + REGIONS - 1)
+        for k in range(1, NY):
+            y_copy(k).start()
+        lax.fori_loop(1, DOMAINS, start(geo_copy), 0)
+        geo_copy(1).wait_recv()
+        prepare(1, 1)
+        push(1, 0)
+        lax.fori_loop(1, 8, block, 0)
         for k in range(1, NY):
             y_copy(k).wait_recv()
         mz_in[0] = mom[...] + my_in[1] + my_in[2] + my_in[3]
         for k in range(1, NZ):
             z_copy(k).start()
-        lax.fori_loop(1, 10, arrived_block, 0)
+        lax.fori_loop(8, 17, block, 0)
         for k in range(1, NZ):
             z_copy(k).wait_recv()
         total = mz_in[0]
@@ -227,7 +261,10 @@
         mall[0, 36:40, :] = jnp.zeros((4, LANES), F32)
         for k in range(1, REGIONS):
             r_copy(k).start()
-        lax.fori_loop(10, DOMAINS, arrived_block, 0)
+        lax.fori_loop(17, DOMAINS - 1, block, 0)
+        push((DOMAINS - 1) % 2, 1)
+        stream(DOMAINS - 1, 0)
+        stream(DOMAINS - 1, 1)
         for c in range(CHUNKS):
             one, three = pltpu.matmul_pop(acc1[c]), pltpu.matmul_pop(acc3[c])
             xb[0, c * CHUNK : (c + 1) * CHUNK, :] = one[:, 0:LANES]
@@ -237,23 +274,14 @@
 
     for k in range(1, REGIONS):
         r_copy(k).wait_recv()
-    at = pl.ds(pl.multiple_of(region * LANES, LANES), LANES)
-    target = jnp.transpose(jnp.concatenate([cen[0:3, at], jnp.zeros((5, LANES), F32)], axis=0))
-    target = [jnp.broadcast_to(target[:, a : a + 1], (LANES, LANES)) for a in range(3)]
-    weights, kernels = [], []
+    steps = []
     for k in range(1, REGIONS):
-        source = pl.ds(pl.multiple_of(((region + REGIONS - k) % REGIONS) * LANES, LANES), LANES)
-        diff = [target[a] - cen[a : a + 1, source] for a in range(3)]
-        g1 = lax.rsqrt(diff[0] * diff[0] + diff[1] * diff[1] + diff[2] * diff[2] + CORE2)
-        g3 = g1 * g1 * g1
         total = mall[k]
-        for p, part in enumerate([g1] + [diff[a] * g3 for a in range(3)]):
-            high, low = split2(part)
+        for p in range(4):
             wh, wl = split2(jnp.concatenate([total[9 * p : 9 * p + 9], jnp.zeros((7, LANES), F32)], axis=0))
             both = jnp.concatenate([wh, wl], axis=0)
-            kernels += [high, low]
-            weights += [both, both]
-    far = dot_nt(jnp.concatenate(weights, axis=1), jnp.concatenate(kernels, axis=1))
+            steps.append((jnp.concatenate([both, both], axis=1), padded(kern[4 * (k - 1) + p]), True))
+    far = mxu_sum(32, steps)
     far = split3(far[0:16, 0:LANES] + far[16:32, 0:LANES])
     cell_hot = (lax.broadcasted_iota(I32, (TILE, SEG), 0) % LANES == cid[...]).astype(F32).astype(BF16)
     pair = [jnp.concatenate(far[0:2], axis=1), jnp.concatenate([far[2], jnp.zeros_like(far[2])], axis=1)]
@@ -342,15 +370,26 @@
 def body(midpoints, line_vectors, burgers, destination, node_ids, cell_ids, cell_centers):
     vmem = pl.BlockSpec(memory_space=pltpu.VMEM)
     dma = pltpu.SemaphoreType.DMA
+    inputs = (midpoints, line_vectors, burgers, destination.reshape(1, SEG), node_ids, cell_ids.reshape(1, SEG), cell_centers)
+    inputs = [pltpu.with_memory_space_constraint(value, pltpu.HBM) for value in inputs]
     return pl.pallas_call(
         kernel,
         out_shape=(jax.ShapeDtypeStruct((3, 2 * SEG), F32), jax.ShapeDtypeStruct((3, 256), F32)),
-        in_specs=[vmem] * 7,
+        in_specs=[pl.BlockSpec(memory_space=pltpu.HBM)] * 7,
         out_specs=(vmem, vmem),
         scratch_shapes=[
+            pltpu.VMEM((3, SEG), F32),
+            pltpu.VMEM((3, SEG), F32),
+            pltpu.VMEM((3, SEG), F32),
+            pltpu.VMEM((1, SEG), I32),
+            pltpu.VMEM((2, SEG), I32),
+            pltpu.VMEM((1, SEG), I32),
+            pltpu.VMEM((3, REGIONS * LANES), F32),
+            dma((7,)),
+            pltpu.VMEM((4 * (REGIONS - 1), LANES, TILE), BF16),
             pltpu.VMEM((DOMAINS, 40, LANES), F32),
             pltpu.VMEM((4, SEG, LANES), F32),
-            pltpu.VMEM((2, 64, LANES), F32),
+            pltpu.VMEM((2, 2, 64, LANES), F32),
             pltpu.VMEM((40, LANES), F32),
             pltpu.VMEM((NY, 40, LANES), F32),
             pltpu.VMEM((NZ, 40, LANES), F32),
@@ -366,9 +405,7 @@
         compiler_params=pltpu.CompilerParams(
             collective_id=0, has_side_effects=True, vmem_limit_bytes=32 << 20
         ),
-    )(
-        midpoints, line_vectors, burgers, destination.reshape(1, SEG), node_ids, cell_ids.reshape(1, SEG), cell_centers
-    )
+    )(*inputs)
 
 
 def solution(mesh):

time: 62.6 us -> 52.8 us (0.84)
  local copies, waits for them, and re-layouts: 6.05 us -> 1.2 us
  Pallas kernels: 55.3 us -> 50.8 us
    unnamed x16 -> x2, local copies, waits for them, and re-layouts: 6.05 us -> 1.2 us
    pallas_call x1, Pallas kernels: 55.3 us -> 50.8 us  [body(): pl.pallas_call(kernel, out_shape=(jax.ShapeDtypeStruct((3, 2 * SEG), F32)...]
where the time goes in v2:
time: 52.8 us; the launch traced here: 52.6 us
  Pallas kernels  50.8 us (96%)
  local copies, waits for them, and re-layouts  1.2 us (2%)
  between operations  0.64 us (1%)
    pallas_call x1, Pallas kernels, body(): pl.pallas_call(kernel, out_shape=(jax.ShapeDtypeStruct((3, 2 * SEG), F32)...  50.8 us
    unnamed x2, local copies, waits for them, and re-layouts  1.2 us

profile of v2, /device:TPU:2, one launch (start us, length us, event | category | flops | bytes accessed | tf_op | source)
XLA Modules:
  0.0 52.6 jit_solution(14950214392771497682)
XLA Ops:
  0.6 50.8 %shard_map.86 = (f32[3,1024]{1,0:T(4,128)S(1)}, f32[3,256]{1,0:T(4,128)S(1)}) custom-call(f32[3,512]{1,0:T(4,128)} %mid_in.1, f32[3,512]{1,0:T(4,128)} %lin_in.1, f32[3,512]{1,0:T(4,128)} %bur_in.1, s32[1,512]{1,0:T(1,128)} %bitcast.2, s32[2,512]{1,0:T(2,128)} %nid_in.1, s32[1,512]{1,0:T(1,128)} %bitcast.3, f32[3,1024]{1,0:T(4,128)} %cen_in.1), custom_call_target="tpu_custom_call" | custom-call | tf_op jit(solution)/shard_map/pallas_call | solution.py:375
  51.4 0.6 %copy.11 = f32[3,1024]{1,0:T(4,128)} copy(f32[3,1024]{1,0:T(4,128)S(1)} %get-tuple-element.4) | data formatting | bytes 24576
  52.0 0.6 %copy.12 = f32[3,256]{1,0:T(4,128)} copy(f32[3,256]{1,0:T(4,128)S(1)} %get-tuple-element.5) | data formatting | bytes 6144

commit v3 on v2

--- a/solution.py
+++ b/solution.py
@@ -54,11 +54,9 @@
     return mxu_sum(left.shape[0], [(left[:, k], padded(right[:, k]), True) for k in tiles])
 
 
-def offset(k, z, y):
-    i = k // NY
+def z_offset(i):
     odd = i % 2
-    dz = odd * ((i + 1) // 2) + (1 - odd) * ((NZ - i // 2) % NZ)
-    return ((z + dz) % NZ) * NY + (y + k % NY) % NY
+    return odd * ((i + 1) // 2) + (1 - odd) * ((NZ - i // 2) % NZ)
 
 
 def kernel(
@@ -122,10 +120,20 @@
             src_ref=mom, dst_ref=my_in.at[k], send_sem=my_send.at[k], recv_sem=my_recv.at[k],
             device_id=(region, z * NY + (y + k) % NY), device_id_type=MESH)
 
-    def geo_copy(k):
+    def geo_copy(source, k, peer):
         return pltpu.make_async_remote_copy(
-            src_ref=geo.at[0], dst_ref=geo.at[k], send_sem=geo_send.at[k], recv_sem=geo_recv.at[k],
-            device_id=(region, offset(k, z, y)), device_id_type=MESH)
+            src_ref=geo.at[source], dst_ref=geo.at[k], send_sem=geo_send.at[k], recv_sem=geo_recv.at[k],
+            device_id=(region, peer), device_id_type=MESH)
+
+    def geo_along_z(i):
+        return geo_copy(0, i, ((z + z_offset(i)) % NZ) * NY + y)
+
+    def geo_along_y(source, step):
+        return geo_copy(source, NZ + (NY - 1) * source + step - 1, z * NY + (y + step) % NY)
+
+    def pass_on(source):
+        for step in range(1, NY):
+            geo_along_y(source, step).start()
 
     def z_copy(k):
         return pltpu.make_async_remote_copy(
@@ -136,6 +144,9 @@
         return pltpu.make_async_remote_copy(
             src_ref=mall.at[0], dst_ref=mall.at[k], send_sem=mr_send.at[k], recv_sem=mr_recv.at[k],
             device_id=((region + k) % REGIONS, dom), device_id_type=MESH)
+
+    def geo_wait(k):
+        return geo_copy(0, k, z * NY + (y + 1) % NY)
 
     def start(copy):
         def run(k, c):
@@ -215,10 +226,12 @@
                 pltpu.matmul_acc_lhs(acc1[c], l1)
                 pltpu.matmul_acc_lhs(acc3[c], l3)
 
-        def block(k, carry):
+        def block(k, carry, passing=False):
             push(k % 2, 1)
             stream(k, 0)
-            geo_copy(k + 1).wait_recv()
+            geo_wait(k + 1).wait_recv()
+            if passing:
+                pass_on(k + 1)
             prepare(k + 1, (k + 1) % 2)
             push((k + 1) % 2, 0)
             stream(k, 1)
@@ -233,17 +246,19 @@
         pl.semaphore_wait(barrier, DOMAINS - 1 + REGIONS - 1)
         for k in range(1, NY):
             y_copy(k).start()
-        lax.fori_loop(1, DOMAINS, start(geo_copy), 0)
-        geo_copy(1).wait_recv()
+        lax.fori_loop(1, NZ, start(geo_along_z), 0)
+        pass_on(0)
+        geo_wait(1).wait_recv()
+        pass_on(1)
         prepare(1, 1)
         push(1, 0)
-        lax.fori_loop(1, 8, block, 0)
+        lax.fori_loop(1, NZ - 1, lambda k, c: block(k, c, True), 0)
         for k in range(1, NY):
             y_copy(k).wait_recv()
         mz_in[0] = mom[...] + my_in[1] + my_in[2] + my_in[3]
         for k in range(1, NZ):
             z_copy(k).start()
-        lax.fori_loop(8, 17, block, 0)
+        lax.fori_loop(NZ - 1, 16, block, 0)
         for k in range(1, NZ):
             z_copy(k).wait_recv()
         total = mz_in[0]
@@ -261,7 +276,7 @@
         mall[0, 36:40, :] = jnp.zeros((4, LANES), F32)
         for k in range(1, REGIONS):
             r_copy(k).start()
-        lax.fori_loop(17, DOMAINS - 1, block, 0)
+        lax.fori_loop(16, DOMAINS - 1, block, 0)
         push((DOMAINS - 1) % 2, 1)
         stream(DOMAINS - 1, 0)
         stream(DOMAINS - 1, 1)
@@ -358,7 +373,7 @@
         for j in range(8):
             slot_out[c : c + 1, j * LANES : (j + 1) * LANES] = line[j : j + 1]
 
-    for copy, count in ((y_copy, NY), (geo_copy, DOMAINS), (z_copy, NZ), (r_copy, REGIONS), (out_copy, DOMAINS)):
+    for copy, count in ((y_copy, NY), (geo_wait, DOMAINS), (z_copy, NZ), (r_copy, REGIONS), (out_copy, DOMAINS)):
 
         def sent(k, c, copy=copy):
             copy(k).wait_send()

time: 52.8 us -> 47.3 us (0.90); the launches traced: 52.6 us -> 46.5 us
  Pallas kernels: 50.8 us -> 44.7 us
    pallas_call x1, Pallas kernels: 50.8 us -> 44.7 us  [body(): pl.pallas_call(kernel, out_shape=(jax.ShapeDtypeStruct((3, 2 * SEG), F32)...]
where the time goes in v3:
time: 47.3 us; the launch traced here: 46.5 us
  Pallas kernels  44.7 us (95%)
  local copies, waits for them, and re-layouts  1.2 us (3%)
  between operations  0.64 us (1%)
    pallas_call x1, Pallas kernels, body(): pl.pallas_call(kernel, out_shape=(jax.ShapeDtypeStruct((3, 2 * SEG), F32)...  44.7 us
    unnamed x2, local copies, waits for them, and re-layouts  1.2 us

profile of v3, /device:TPU:2, one launch (start us, length us, event | category | flops | bytes accessed | tf_op | source)
XLA Modules:
  0.0 46.5 jit_solution(14685882523423847869)
XLA Ops:
  0.6 44.7 %shard_map.86 = (f32[3,1024]{1,0:T(4,128)S(1)}, f32[3,256]{1,0:T(4,128)S(1)}) custom-call(f32[3,512]{1,0:T(4,128)} %mid_in.1, f32[3,512]{1,0:T(4,128)} %lin_in.1, f32[3,512]{1,0:T(4,128)} %bur_in.1, s32[1,512]{1,0:T(1,128)} %bitcast.2, s32[2,512]{1,0:T(2,128)} %nid_in.1, s32[1,512]{1,0:T(1,128)} %bitcast.3, f32[3,1024]{1,0:T(4,128)} %cen_in.1), custom_call_target="tpu_custom_call" | custom-call | tf_op jit(solution)/shard_map/pallas_call | solution.py:390
  45.3 0.6 %copy.11 = f32[3,1024]{1,0:T(4,128)} copy(f32[3,1024]{1,0:T(4,128)S(1)} %get-tuple-element.4) | data formatting | bytes 24576
  45.9 0.6 %copy.12 = f32[3,256]{1,0:T(4,128)} copy(f32[3,256]{1,0:T(4,128)S(1)} %get-tuple-element.5) | data formatting | bytes 6144

commit v4 on v3

--- a/solution.py
+++ b/solution.py
@@ -226,13 +226,54 @@
                 pltpu.matmul_acc_lhs(acc1[c], l1)
                 pltpu.matmul_acc_lhs(acc3[c], l3)
 
-        def block(k, carry, passing=False):
+        def column_moments():
+            for k in range(1, NY):
+                y_copy(k).wait_recv()
+            mz_in[0] = mom[...] + my_in[1] + my_in[2] + my_in[3]
+            for k in range(1, NZ):
+                z_copy(k).start()
+
+        def region_moments():
+            for k in range(1, NZ):
+                z_copy(k).wait_recv()
+            total = mz_in[0]
+            for k in range(1, NZ):
+                total = total + mz_in[k]
+            center = [cen[a : a + 1, pl.ds(pl.multiple_of(region * LANES, LANES), LANES)] - middle[a] for a in range(3)]
+            mall[0, 0:9, :] = total[0:9]
+            for a in range(3):
+                for k in range(9):
+                    at = 9 + 9 * a + k
+                    value = total[at : at + 1] - center[a] * total[k : k + 1]
+                    if k % 3 == a:
+                        value = value + total[36 + k // 3 : 37 + k // 3]
+                    mall[0, at : at + 1, :] = value
+            mall[0, 36:40, :] = jnp.zeros((4, LANES), F32)
+            for k in range(1, REGIONS):
+                r_copy(k).start()
+
+        def block(k, carry):
             push(k % 2, 1)
             stream(k, 0)
-            geo_wait(k + 1).wait_recv()
-            if passing:
-                pass_on(k + 1)
-            prepare(k + 1, (k + 1) % 2)
+            later = (k + 1) - (k + 1) // DOMAINS
+
+            @pl.when(k < DOMAINS - 1)
+            def _():
+                geo_wait(later).wait_recv()
+
+            @pl.when(k < NZ - 1)
+            def _():
+                pass_on(later)
+
+            @pl.when(k == NZ - 2)
+            def _():
+                column_moments()
+
+            @pl.when(k == 15)
+            def _():
+                region_moments()
+
+            prepare(later, (k + 1) % 2)
             push((k + 1) % 2, 0)
             stream(k, 1)
             return carry
@@ -244,42 +285,17 @@
         stream(0, 1)
 
         pl.semaphore_wait(barrier, DOMAINS - 1 + REGIONS - 1)
+        lax.fori_loop(1, NZ, start(geo_along_z), 0)
         for k in range(1, NY):
             y_copy(k).start()
-        lax.fori_loop(1, NZ, start(geo_along_z), 0)
         pass_on(0)
         geo_wait(1).wait_recv()
         pass_on(1)
         prepare(1, 1)
         push(1, 0)
-        lax.fori_loop(1, NZ - 1, lambda k, c: block(k, c, True), 0)
-        for k in range(1, NY):
-            y_copy(k).wait_recv()
-        mz_in[0] = mom[...] + my_in[1] + my_in[2] + my_in[3]
-        for k in range(1, NZ):
-            z_copy(k).start()
-        lax.fori_loop(NZ - 1, 16, block, 0)
-        for k in range(1, NZ):
-            z_copy(k).wait_recv()
-        total = mz_in[0]
-        for k in range(1, NZ):
-            total = total + mz_in[k]
-        center = [cen[a : a + 1, pl.ds(pl.multiple_of(region * LANES, LANES), LANES)] - middle[a] for a in range(3)]
-        mall[0, 0:9, :] = total[0:9]
-        for a in range(3):
-            for k in range(9):
-                at = 9 + 9 * a + k
-                value = total[at : at + 1] - center[a] * total[k : k + 1]
-                if k % 3 == a:
-                    value = value + total[36 + k // 3 : 37 + k // 3]
-                mall[0, at : at + 1, :] = value
-        mall[0, 36:40, :] = jnp.zeros((4, LANES), F32)
-        for k in range(1, REGIONS):
-            r_copy(k).start()
-        lax.fori_loop(16, DOMAINS - 1, block, 0)
-        push((DOMAINS - 1) % 2, 1)
-        stream(DOMAINS - 1, 0)
-        stream(DOMAINS - 1, 1)
+        lax.fori_loop(1, DOMAINS, block, 0)
+        pltpu.matmul_acc_lhs(acc1[0], jnp.zeros((CHUNK, TILE), BF16), 0)
+        pltpu.matmul_acc_lhs(acc3[0], jnp.zeros((CHUNK, TILE), BF16), 0)
         for c in range(CHUNKS):
             one, three = pltpu.matmul_pop(acc1[c]), pltpu.matmul_pop(acc3[c])
             xb[0, c * CHUNK : (c + 1) * CHUNK, :] = one[:, 0:LANES]
@@ -341,7 +357,7 @@
     msg[pl.ds(6, DOMAINS, stride=8), :] = slots
 
     def out_copy(k):
-        peer = (dom + k) % DOMAINS
+        peer = (dom + DOMAINS // 2 + (k % 2) * (k // 2) + (1 - k % 2) * (DOMAINS - k // 2)) % DOMAINS
         return pltpu.make_async_remote_copy(
             src_ref=msg.at[pl.ds(pl.multiple_of(8 * peer, 8), 8), :],
             dst_ref=arrived.at[pl.ds(pl.multiple_of(8 * dom, 8), 8), :],

time: 47.3 us -> 46.7 us (0.987); the launches traced: 46.5 us -> 46.5 us
  no operation moved by 1% of the time
where the time goes in v4:
time: 46.7 us; the launch traced here: 46.5 us
  Pallas kernels  44.7 us (96%)
  local copies, waits for them, and re-layouts  1.2 us (3%)
  between operations  0.64 us (1%)
    pallas_call x1, Pallas kernels, body(): pl.pallas_call(kernel, out_shape=(jax.ShapeDtypeStruct((3, 2 * SEG), F32)...  44.7 us
    unnamed x2, local copies, waits for them, and re-layouts  1.2 us

profile of v4, /device:TPU:2, one launch (start us, length us, event | category | flops | bytes accessed | tf_op | source)
XLA Modules:
  0.0 46.5 jit_solution(226462624006305141)
XLA Ops:
  0.6 44.7 %shard_map.86 = (f32[3,1024]{1,0:T(4,128)S(1)}, f32[3,256]{1,0:T(4,128)S(1)}) custom-call(f32[3,512]{1,0:T(4,128)} %mid_in.1, f32[3,512]{1,0:T(4,128)} %lin_in.1, f32[3,512]{1,0:T(4,128)} %bur_in.1, s32[1,512]{1,0:T(1,128)} %bitcast.2, s32[2,512]{1,0:T(2,128)} %nid_in.1, s32[1,512]{1,0:T(1,128)} %bitcast.3, f32[3,1024]{1,0:T(4,128)} %cen_in.1), custom_call_target="tpu_custom_call" | custom-call | tf_op jit(solution)/shard_map/pallas_call | solution.py:406
  45.3 0.6 %copy.11 = f32[3,1024]{1,0:T(4,128)} copy(f32[3,1024]{1,0:T(4,128)S(1)} %get-tuple-element.4) | data formatting | bytes 24576
  45.9 0.6 %copy.12 = f32[3,256]{1,0:T(4,128)} copy(f32[3,256]{1,0:T(4,128)S(1)} %get-tuple-element.5) | data formatting | bytes 6144

commit v5 on v4

--- a/solution.py
+++ b/solution.py
@@ -207,7 +207,7 @@
             for w in range(2):
                 wide = jnp.concatenate([wsc[slot, w, pl.ds(2 * t + u, 16, stride=4), :] for u in range(2)], axis=1)
                 high, low = split2(wide)
-                pltpu.matmul_push_rhs(jnp.concatenate([high, low, blank], axis=0), t, w, transpose=True)
+                pltpu.matmul_push_rhs(jnp.concatenate([high, low, blank] if w == 0 else [blank[0:32], high, low, blank[32:]], axis=0), t, w, transpose=True)
 
         def stream(k, t):
             s = [
@@ -298,8 +298,7 @@
         pltpu.matmul_acc_lhs(acc3[0], jnp.zeros((CHUNK, TILE), BF16), 0)
         for c in range(CHUNKS):
             one, three = pltpu.matmul_pop(acc1[c]), pltpu.matmul_pop(acc3[c])
-            xb[0, c * CHUNK : (c + 1) * CHUNK, :] = one[:, 0:LANES]
-            xb[1, c * CHUNK : (c + 1) * CHUNK, :] = three[:, 0:LANES]
+            xb[0, c * CHUNK : (c + 1) * CHUNK, :] = one[:, 0:LANES] + three[:, 0:LANES]
 
     pl.run_scoped(pairs, *[pltpu.ACC(w)((CHUNK, TILE), F32) for w in range(2) for _ in range(CHUNKS)])
 
@@ -320,9 +319,8 @@
         [mxu_sum(16, [(left, cell_hot[:, k : k + TILE], False) for left in pair]) for k in (0, TILE)], axis=1
     )
 
-    one, three = jnp.transpose(xb[0]), jnp.transpose(xb[1])
-    one = one[0:16] + one[16:32]
-    three = three[0:16] + three[16:32]
+    sums = jnp.transpose(xb[0])
+    one, three = sums[0:16] + sums[16:32], sums[32:48] + sums[48:64]
     x = [mid[a : a + 1, :] - middle[a] for a in range(3)]
     b = rows_of(bur)
     stress = [

time: 46.7 us -> 46.5 us (level)
  no operation moved by 1% of the time
where the time goes in v5:
time: 46.5 us; the launch traced here: 46.4 us
  Pallas kernels  44.5 us (96%)
  local copies, waits for them, and re-layouts  1.2 us (3%)
  between operations  0.64 us (1%)
    pallas_call x1, Pallas kernels, body(): pl.pallas_call(kernel, out_shape=(jax.ShapeDtypeStruct((3, 2 * SEG), F32)...  44.5 us
    unnamed x2, local copies, waits for them, and re-layouts  1.2 us

profile of v5, /device:TPU:2, one launch (start us, length us, event | category | flops | bytes accessed | tf_op | source)
XLA Modules:
  0.0 46.4 jit_solution(17839533542159780726)
XLA Ops:
  0.6 44.5 %shard_map.86 = (f32[3,1024]{1,0:T(4,128)S(1)}, f32[3,256]{1,0:T(4,128)S(1)}) custom-call(f32[3,512]{1,0:T(4,128)} %mid_in.1, f32[3,512]{1,0:T(4,128)} %lin_in.1, f32[3,512]{1,0:T(4,128)} %bur_in.1, s32[1,512]{1,0:T(1,128)} %bitcast.2, s32[2,512]{1,0:T(2,128)} %nid_in.1, s32[1,512]{1,0:T(1,128)} %bitcast.3, f32[3,1024]{1,0:T(4,128)} %cen_in.1), custom_call_target="tpu_custom_call" | custom-call | tf_op jit(solution)/shard_map/pallas_call | solution.py:404
  45.2 0.6 %copy.11 = f32[3,1024]{1,0:T(4,128)} copy(f32[3,1024]{1,0:T(4,128)S(1)} %get-tuple-element.4) | data formatting | bytes 24576
  45.8 0.6 %copy.12 = f32[3,256]{1,0:T(4,128)} copy(f32[3,256]{1,0:T(4,128)S(1)} %get-tuple-element.5) | data formatting | bytes 6144

commit v6 on v5

--- a/solution.py
+++ b/solution.py
@@ -366,6 +366,14 @@
     mine = pl.ds(pl.multiple_of(8 * dom, 8), 8)
     arrived[mine, :] = msg[mine, :]
 
+    for copy, count in ((y_copy, NY), (geo_wait, DOMAINS), (z_copy, NZ), (r_copy, REGIONS), (out_copy, DOMAINS)):
+
+        def sent(k, c, copy=copy):
+            copy(k).wait_send()
+            return c
+
+        lax.fori_loop(1, count, sent, 0)
+
     def received(k, c):
         out_copy(k).wait_recv()
         return c
@@ -386,14 +394,6 @@
             line = jnp.where(quarter == a, pltpu.roll(four[a], turn, 1) if turn else four[a], line)
         for j in range(8):
             slot_out[c : c + 1, j * LANES : (j + 1) * LANES] = line[j : j + 1]
-
-    for copy, count in ((y_copy, NY), (geo_wait, DOMAINS), (z_copy, NZ), (r_copy, REGIONS), (out_copy, DOMAINS)):
-
-        def sent(k, c, copy=copy):
-            copy(k).wait_send()
-            return c
-
-        lax.fori_loop(1, count, sent, 0)
 
 
 def body(midpoints, line_vectors, burgers, destination, node_ids, cell_ids, cell_centers):

time: 46.5 us -> 46 us (0.989)
  Pallas kernels: 44.5 us -> 44 us
    pallas_call x1, Pallas kernels: 44.5 us -> 44 us  [body(): pl.pallas_call(kernel, out_shape=(jax.ShapeDtypeStruct((3, 2 * SEG), F32)...]
where the time goes in v6:
time: 46 us; the launch traced here: 45.9 us
  Pallas kernels  44 us (96%)
  local copies, waits for them, and re-layouts  1.2 us (3%)
  between operations  0.64 us (1%)
    pallas_call x1, Pallas kernels, body(): pl.pallas_call(kernel, out_shape=(jax.ShapeDtypeStruct((3, 2 * SEG), F32)...  44 us
    unnamed x2, local copies, waits for them, and re-layouts  1.2 us

profile of v6, /device:TPU:2, one launch (start us, length us, event | category | flops | bytes accessed | tf_op | source)
XLA Modules:
  0.0 45.9 jit_solution(9544139019027464728)
XLA Ops:
  0.6 44.0 %shard_map.86 = (f32[3,1024]{1,0:T(4,128)S(1)}, f32[3,256]{1,0:T(4,128)S(1)}) custom-call(f32[3,512]{1,0:T(4,128)} %mid_in.1, f32[3,512]{1,0:T(4,128)} %lin_in.1, f32[3,512]{1,0:T(4,128)} %bur_in.1, s32[1,512]{1,0:T(1,128)} %bitcast.2, s32[2,512]{1,0:T(2,128)} %nid_in.1, s32[1,512]{1,0:T(1,128)} %bitcast.3, f32[3,1024]{1,0:T(4,128)} %cen_in.1), custom_call_target="tpu_custom_call" | custom-call | tf_op jit(solution)/shard_map/pallas_call | solution.py:404
  44.7 0.6 %copy.11 = f32[3,1024]{1,0:T(4,128)} copy(f32[3,1024]{1,0:T(4,128)S(1)} %get-tuple-element.4) | data formatting | bytes 24576
  45.3 0.6 %copy.12 = f32[3,256]{1,0:T(4,128)} copy(f32[3,256]{1,0:T(4,128)S(1)} %get-tuple-element.5) | data formatting | bytes 6144
